TPU v7x, 128 devices: a whole 4x4x4 slice. The times are simulated.
128 devices in a mesh: dp: 16 (over z, x), tm: 8 (over y, core).
Axes of the slice: x: 4, y: 4, z: 4, core: 2. Of those that a mesh axis runs over, the one named last changes fastest.
Arguments:
- frames: bfloat16 [16, 6144, 1024], P('dp', 'tm'), may hold values from -18 to 18
- lengths: int32 [16], P('dp'), may hold values from 1 to 6144, 58982 in all
- w_in: bfloat16 [1024, 2048], replicated, may hold values from -4 to 4
- w_dw: float32 [31, 1024], replicated, may hold values from -1 to 1
- bn_gain: float32 [1024], replicated, may hold values from 0.25 to 1.75
- bn_bias: float32 [1024], replicated, may hold values from -1 to 1
- w_out: bfloat16 [1024, 1024], replicated, may hold values from -0.1875 to 0.1875
- cotangent: bfloat16 [16, 6144, 1024], P('dp', 'tm'), may hold values from -6 to 6
Outputs:
- output: bfloat16 [16, 6144, 1024], P('dp', 'tm')
- grad_frames: bfloat16 [16, 6144, 1024], P('dp', 'tm')
- grad_w_in: float32 [1024, 2048], P(('dp', 'tm'))
- grad_w_out: float32 [1024, 1024], P(('dp', 'tm'))
- grad_kernel: float32 [31, 1024], replicated
- grad_gain: float32 [1024], replicated
- grad_bias: float32 [1024], replicated
Inputs may be any that keep to these rules, and one draw needn't show every extreme that they name: Frame slots at or after a recording's length are padding; the lengths sum to 58982 and the longest is exactly 6144.
All inputs are finite; a program needn't handle non-finite values. No bound on the sum of `lengths` on one device may be relied on, other than what follows from the above.
Results may differ from a plain program's by a relative error of at most 0.015.
Values may be sent and summed in bfloat16 or wider, within the bound.
A program may use at most 128 MiB of HBM per device.

v0:
```python
import math
import jax
import jax.numpy as jnp
from jax import lax
from jax.sharding import PartitionSpec as P


def padded_2(cells, sides, width):
    for axis, dim in sides:
        count = lax.axis_size(axis)
        ends = count - 1
        head = lax.slice_in_dim(cells, 0, width, axis=dim)
        tail = lax.slice_in_dim(cells, cells.shape[dim] - width, cells.shape[dim], axis=dim)
        cells = jnp.concatenate(
            [
                lax.ppermute(tail, axis, [(i, (i + 1) % count) for i in range(ends)]),
                cells,
                lax.ppermute(head, axis, [((i + 1) % count, i) for i in range(ends)]),
            ],
            axis=dim,
        )
    return cells


def taps_forward(padded, kernel, frame_count):
    summed = jnp.zeros((frame_count, padded.shape[1]), jnp.float32)
    for tap_index in range(kernel.shape[0]):
        summed = summed + kernel[tap_index] * padded[tap_index : tap_index + frame_count].astype(
            jnp.float32
        )
    return summed


def taps_backward(padded_grad, kernel, frame_count):
    reach_both = kernel.shape[0] - 1
    summed = jnp.zeros((frame_count, padded_grad.shape[1]), jnp.float32)
    for tap_index in range(kernel.shape[0]):
        begin = reach_both - tap_index
        summed = summed + kernel[tap_index] * padded_grad[begin : begin + frame_count].astype(
            jnp.float32
        )
    return summed


def taps_kernel(padded_glu, dconv_rows, kernel_taps, frame_count):
    grad_rows = dconv_rows.astype(jnp.float32)
    tap_rows = []
    for tap_index in range(kernel_taps):
        tap_rows.append(
            jnp.sum(
                padded_glu[tap_index : tap_index + frame_count].astype(jnp.float32) * grad_rows,
                axis=0,
            )
        )
    return jnp.stack(tap_rows)


def row_product(left_rows, right_mat, contract):
    dim_spec = (((1,), (contract,)), ((), ()))
    return lax.dot_general(left_rows, right_mat, dim_spec, preferred_element_type=jnp.float32)


def local(frames, lengths, w_in, w_dw, bn_gain, bn_bias, w_out, cotangent):
    frame_rows = frames.shape[1]
    channels = frames.shape[2]
    kernel_taps = w_dw.shape[0]
    reach = (kernel_taps - 1) // 2
    feats = frames[0]
    cot_rows = cotangent[0]
    tm_count = lax.axis_size("tm")
    device_count = lax.axis_size("dp") * tm_count
    offset = lax.axis_index("tm") * frame_rows
    limit = lengths[0]
    positions = offset + jnp.arange(frame_rows, dtype=jnp.int32)
    live_rows = (positions < limit).astype(jnp.float32)[:, None]
    contract_frames = (((0,), (0,)), ((), ()))
    pre_act = row_product(feats, w_in, 0)
    linear_half = pre_act[:, :channels]
    gate_sig = jax.nn.sigmoid(pre_act[:, channels:])
    glu_out = (linear_half * gate_sig * live_rows).astype(jnp.bfloat16)
    dswish = row_product(cot_rows, w_out, 1)
    padded = padded_2(glu_out, (("tm", 0),), reach)
    conv_out = taps_forward(padded, w_dw, frame_rows)
    local_sum = jnp.sum(conv_out * live_rows, axis=0)
    local_sq = jnp.sum(conv_out * conv_out * live_rows, axis=0)
    local_count = jnp.sum(live_rows)
    sums, squares, count = lax.psum((local_sum, local_sq, local_count), ("dp", "tm"))
    mean_vec = sums / count
    variance = squares / count - mean_vec * mean_vec
    inv_std = lax.rsqrt(variance + 1e-05)
    normed = (conv_out - mean_vec) * inv_std
    shifted = bn_gain * normed + bn_bias
    act_sig = jax.nn.sigmoid(shifted)
    swished = (shifted * act_sig * live_rows).astype(jnp.bfloat16)
    dshift = live_rows * dswish * act_sig * (1.0 + shifted * (1.0 - act_sig))
    sum_gain, sum_bias = lax.psum(
        (jnp.sum(dshift * normed, axis=0), jnp.sum(dshift, axis=0)), ("dp", "tm")
    )
    dconv = (
        live_rows * bn_gain * inv_std * (dshift - sum_bias / count - normed * sum_gain / count)
    ).astype(jnp.bfloat16)
    padded_grad = padded_2(dconv, (("tm", 0),), reach)
    dglu = live_rows * taps_backward(padded_grad, w_dw, frame_rows)
    kernel_sum = lax.psum(taps_kernel(padded, dconv, kernel_taps, frame_rows), ("dp", "tm"))
    out_rows = row_product(swished, w_out, 0).astype(jnp.bfloat16)
    dpre = jnp.concatenate(
        [dglu * gate_sig, dglu * linear_half * gate_sig * (1.0 - gate_sig)], axis=1
    ).astype(jnp.bfloat16)
    grad_rows = row_product(dpre, w_in, 1).astype(jnp.bfloat16)
    term_in = lax.dot_general(feats, dpre, contract_frames, preferred_element_type=jnp.float32)
    term_out = lax.dot_general(
        swished, cot_rows, contract_frames, preferred_element_type=jnp.float32
    )
    weight_term = jnp.concatenate([term_in, term_out], axis=1)
    weight_sum = lax.psum_scatter(weight_term, ("dp", "tm"), scatter_dimension=0, tiled=True)
    scale = 1.0 / math.sqrt(device_count * frame_rows)
    grad_w_in = weight_sum[:, : 2 * channels] * scale
    grad_w_out = weight_sum[:, 2 * channels :] * scale
    return (
        out_rows[None],
        grad_rows[None],
        grad_w_in,
        grad_w_out,
        kernel_sum * scale,
        sum_gain * scale,
        sum_bias * scale,
    )


def solution(mesh):
    placed = (P("dp", "tm", None), P("dp"), P(), P(), P(), P(), P(), P("dp", "tm", None))
    return jax.shard_map(
        local,
        mesh=mesh,
        in_specs=placed,
        out_specs=(
            P("dp", "tm", None),
            P("dp", "tm", None),
            P(("dp", "tm"), None),
            P(("dp", "tm"), None),
            P(),
            P(),
            P(),
        ),
        check_vma=False,
    )
```

profile of v0, /device:TPU:0, one launch (start us, length us, event | category | flops | bytes accessed | tf_op | source)
XLA Modules:
  0.0 603.7 jit_solution(6638876811179374699)
XLA Ops:
  8.0 5.7 fusion.143
  14.6 1.8 copy-done.4
  16.4 1.4 collective-permute-start
  17.8 1.3 collective-permute-start.1
  19.8 3.0 collective-permute-done.1
  22.8 24.4 %multiply_reduce_fusion.2 = (f32[1024]{0:T(1024)S(1)}, f32[1024]{0:T(1024)S(1)}, f32[768,1024]{1,0:T(8,128)}) fusion(f32[768]{0:T(1024)S(1)} %fusion.147, bf16[15,1024]{1,0:T(8,128)(2,1)S(1)} %collective-permute-done.1, bf16[768,1024]{1,0:T(8,128)(2,1)S(1)} %multiply_convert_fusion.4, f32[1024]{0:T(1024)S(1)} %bitcast.146, f32[1024]{0:T(1024)S(1)} %bitcast.148, ...), kind=kLoop, calls=%fused_computation.213 | loop fusion | flops 147060736 | bytes 4918272 | tf_op jit(solution)/shard_map/reduce_sum | solution.py:84
  47.2 69.6 %all-reduce.1 = (f32[1024]{0:T(1024)S(1)}, f32[]{:T(128)}, f32[1024]{0:T(1024)S(1)}) all-reduce(f32[1024]{0:T(1024)S(1)} %get-tuple-element.52, f32[]{:T(128)} %fusion.148, f32[1024]{0:T(1024)S(1)} %get-tuple-element.51), channel_id=1, replica_groups=mesh['dp'=16,'tm'=8] {'dp','tm'}, use_global_device_ids=true, to_apply=%region_5.0 | all-reduce | flops 2049 | bytes 16392 | tf_op jit(solution)/shard_map/psum | solution.py:87
  117.6 6.4 %fusion.151 = (f32[1024]{0:T(1024)S(1)}, f32[1024]{0:T(1024)S(1)}, f32[768,1024]{1,0:T(8,128)}) fusion(f32[1024]{0:T(1024)S(1)} %get-tuple-element.106, f32[768,1024]{1,0:T(8,128)} %get-tuple-element.67, f32[1024]{0:T(1024)S(1)} %get-tuple-element.105, f32[1024]{0:T(1024)S(1)} %copy-done.16, f32[1024]{0:T(1024)S(1)} %copy-done.12, ...), kind=kOutput, calls=%fused_computation.316 | convolution fusion | flops 1623193600 | bytes 9989120 | tf_op jit(solution)/shard_map/dot_general | solution.py:60
  124.0 63.8 %all-reduce = (f32[1024]{0:T(1024)S(1)}, f32[1024]{0:T(1024)S(1)}) all-reduce(f32[1024]{0:T(1024)S(1)} %get-tuple-element.58, f32[1024]{0:T(1024)S(1)} %get-tuple-element.57), channel_id=1, replica_groups=mesh['dp'=16,'tm'=8] {'dp','tm'}, use_global_device_ids=true, to_apply=%region_9.0 | all-reduce | flops 2048 | bytes 16384 | tf_op jit(solution)/shard_map/psum | solution.py:96
  187.8 1.2 broadcast_multiply_fusion.3
  189.0 15.0 %fusion.75 = (f32[1024]{0:T(1024)S(1)}, f32[1024]{0:T(1024)S(1)}, f32[1024]{0:T(1024)S(1)}, f32[1024]{0:T(1024)S(1)}, f32[1024]{0:T(1024)S(1)}, /*index=5*/f32[1024]{0:T(1024)S(1)}, bf16[768,1024]{1,0:T(8,128)(2,1)S(1)}) fusion(bf16[15,1024]{1,0:T(8,128)(2,1)S(1)} %collective-permute-done.1, bf16[768,1024]{1,0:T(8,128)(2,1)} %copy-done.1, ...), kind=kLoop, calls=%fused_computation.196 | loop fusion | flops 36956160 | bytes 9516036 | tf_op jit(solution)/shard_map/reduce_sum | solution.py:50
  204.1 1.3 collective-permute-start.2
  205.4 3.0 collective-permute-start.3
  208.4 2.7 fusion.60
  211.1 3.2 fusion.74
  214.4 2.9 fusion.59
  217.3 3.7 fusion.76
  221.0 4.5 fusion.139
  225.5 2.7 stack.127
  228.2 40.0 %multiply_convert_fusion.1 = (bf16[768,1024]{1,0:T(8,128)(2,1)S(1)}, f32[768,1024]{1,0:T(8,128)S(1)}) fusion(f32[768,2048]{1,0:T(8,128)} %copy-done.4, bf16[768,1024]{1,0:T(8,128)(2,1)} %copy-done.3, bf16[15,1024]{1,0:T(8,128)(2,1)S(1)} %collective-permute-done.3, f32[1024]{0:T(1024)S(1)} %bitcast.147, f32[1024]{0:T(1024)S(1)} %bitcast.149, ...), kind=kLoop, calls=%fused_computation.204 | loop fusion | flops 147849216 | bytes 9628672 | tf_op jit(solution)/shard_map/convert
  268.2 4.7 multiply_convert_fusion
  273.0 3.5 convolution_bitcast_fusion
  276.5 8.0 %pad_maximum_fusion = f32[1024,3072]{0,1:T(8,128)} fusion(f32[1024,1024]{0,1:T(8,128)S(1)} %copy-done.6, f32[1024,2048]{0,1:T(8,128)S(1)} %convolution_bitcast_fusion), kind=kLoop, calls=%fused_computation.32 | loop fusion | flops 3145728 | bytes 25165824 | tf_op jit(solution)/shard_map/concatenate | solution.py:114
  284.5 12.6 %copy.19 = f32[1024,3072]{1,0:T(8,128)} copy(f32[1024,3072]{0,1:T(8,128)} %pad_maximum_fusion) | data formatting | bytes 25165824
  297.7 5.4 fusion.146
  303.1 4.6 fusion.145
  307.6 58.1 %all-reduce.4.cloned.1.call-done = f32[31,1024]{1,0:T(8,128)} async-done(((f32[31,1024]{1,0:T(8,128)}), f32[31,1024]{1,0:T(8,128)}) %all-reduce.4.cloned.1.call-update) | async-done | bytes 126992 | tf_op jit(solution)/shard_map/psum | solution.py:104
  365.8 1.6 broadcast_multiply_fusion.2
  367.4 223.3 %reduce-scatter.4.cloned.1.call-done = f32[8,3072]{1,0:T(8,128)} async-done(((f32[1024,3072]{1,0:T(8,128)}), f32[8,3072]{1,0:T(8,128)}) %reduce-scatter.4.cloned.1.call-update) | async-done | bytes 98320
  592.4 0.8 slice.635
  593.6 1.1 broadcast_multiply_fusion
  594.7 2.2 copy.17
  (54 shorter events, 5.1 us)
Async XLA Ops:
  7.2 110.4 %copy-start = (bf16[1024,1024]{1,0:T(8,128)(2,1)S(1)}, bf16[1024,1024]{1,0:T(8,128)(2,1)}, u32[]{:S(2)}) copy-start(bf16[1024,1024]{1,0:T(8,128)(2,1)} %param.14) | copy-start | bytes 6291460
  7.2 358.6 %all-reduce.4.cloned.1.call-start = ((), (), s32[]{:S(2)}) async-start(), calls=%async_computation.1 | async-start | bytes 262144 | tf_op jit(solution)/shard_map/psum | solution.py:104
  13.7 2.7 copy-start.4
  13.7 5.4 copy-start.11
  16.4 6.4 %copy-start.1 = (bf16[768,1024]{1,0:T(8,128)(2,1)}, bf16[768,1024]{1,0:T(8,128)(2,1)S(1)}, u32[]{:S(2)}) copy-start(bf16[768,1024]{1,0:T(8,128)(2,1)S(1)} %multiply_convert_fusion.4) | copy-start | bytes 4718596
  16.4 101.2 %copy-start.12 = (f32[1024]{0:T(1024)S(1)}, f32[1024]{0:T(1024)}, u32[]{:S(2)}) copy-start(f32[1024]{0:T(1024)} %param.12) | copy-start | bytes 12292
  16.4 101.2 %copy-start.16 = (f32[1024]{0:T(1024)S(1)}, f32[1024]{0:T(1024)}, u32[]{:S(2)}) copy-start(f32[1024]{0:T(1024)} %param.13) | copy-start | bytes 12292
  16.4 3.5 collective-permute-start
  17.8 5.0 collective-permute-start.1
  189.0 19.4 %copy-start.2 = (bf16[768,1024]{1,0:T(8,128)(2,1)S(1)}, bf16[768,1024]{1,0:T(8,128)(2,1)}, u32[]{:S(2)}) copy-start(bf16[768,1024]{1,0:T(8,128)(2,1)} %copy-done.1) | copy-start | bytes 4718596
  204.0 13.2 %copy-start.3 = (bf16[768,1024]{1,0:T(8,128)(2,1)}, bf16[768,1024]{1,0:T(8,128)(2,1)S(1)}, u32[]{:S(2)}) copy-start(bf16[768,1024]{1,0:T(8,128)(2,1)S(1)} %get-tuple-element.64) | copy-start | bytes 4718596
  204.1 24.1 %collective-permute-start.2 = (bf16[15,1024]{1,0:T(8,128)(2,1)S(1)}, bf16[15,1024]{1,0:T(8,128)(2,1)S(1)}, u32[]{:S(2)}, u32[]{:S(2)}) collective-permute-start(bf16[15,1024]{1,0:T(8,128)(2,1)S(1)} %get-tuple-element.68), channel_id=1, source_target_pairs={{1,0},{2,1},{3,2},{4,3},{5,4},{6,5},{7,6},{9,8},{10,9},{11,10},{12... | collective-permute-start | bytes 92168 | tf_op jit(solution)/shard_map/ppermute | solution.py:18
  205.4 22.8 %collective-permute-start.3 = (bf16[15,1024]{1,0:T(8,128)(2,1)S(1)}, bf16[15,1024]{1,0:T(8,128)(2,1)S(1)}, u32[]{:S(2)}, u32[]{:S(2)}) collective-permute-start(bf16[15,1024]{1,0:T(8,128)(2,1)S(1)} %get-tuple-element.69), channel_id=1, source_target_pairs={{0,1},{1,2},{2,3},{3,4},{4,5},{5,6},{6,7},{8,9},{9,10},{10,11},{11... | collective-permute-start | bytes 92168 | tf_op jit(solution)/shard_map/ppermute | solution.py:16
  214.3 6.6 %copy-start.5 = (f32[768,1024]{1,0:T(8,128)S(1)}, f32[768,1024]{1,0:T(8,128)}, u32[]{:S(2)}) copy-start(f32[768,1024]{1,0:T(8,128)} %get-tuple-element.67) | copy-start | bytes 9437188
  214.3 6.6 %copy-start.14 = (bf16[1,768,1024]{2,1,0:T(8,128)(2,1)S(1)}, bf16[1,768,1024]{2,1,0:T(8,128)(2,1)}, u32[]{:S(2)}) copy-start(bf16[1,768,1024]{2,1,0:T(8,128)(2,1)} %param.15) | copy-start | bytes 4718596
  228.1 362.5 %reduce-scatter.4.cloned.1.call-start = ((), (), s32[]{:S(2)}) async-start(), calls=%async_computation.2 | async-start | bytes 12681216
  268.2 4.7 copy-start.7
  268.2 4.7 copy-start.15
  272.9 3.5 copy-start.9
  272.9 3.5 copy-start.6
  297.7 5.4 copy-start.8
  297.7 5.4 copy-start.10
  297.7 5.4 copy-start.13
Sparse Core Ops, SparseCore 0:
  228.3 137.4 all-reduce.3
  371.5 219.0 reduce-scatter.3
where the time goes:
time: 604 us
  waiting for transfers between devices  284 us (47%)
  blocking collectives  133 us (22%)
  other arithmetic  111 us (18%)
  matrix products  30 us (5%)
  local copies, waits for them, and re-layouts  22.3 us (4%)
  between operations  15.2 us (3%)
  starting transfers between devices  7.12 us (1%)
    unnamed x3, waiting for transfers between devices  223 us
    psum x1, blocking collectives, local(): lax.psum((local_sum, local_sq, local_count), ('dp', 'tm'))  69.6 us
    psum x1, blocking collectives, local(): lax.psum((jnp.sum(dshift * normed, axis=0), jnp.sum(dshift, axis=0)), ('d...  63.8 us
    psum x1, waiting for transfers between devices, local(): lax.psum(taps_kernel(padded, dconv, kernel_taps, frame_rows), ('dp', 'tm'))  58.1 us
    another operation x2, other arithmetic  44.7 us
    reduce_sum x5, other arithmetic, taps_kernel(): jnp.sum(padded_glu[tap_index:tap_index + frame_count].astype(jnp.float32)...  27.5 us
    reduce_sum x1, other arithmetic, local(): local_sum = jnp.sum(conv_out * live_rows, axis=0)  24.4 us
    dot_general x4, matrix products, row_product(): lax.dot_general(left_rows, right_mat, dim_spec, preferred_element_type=jn...  22 us
  transfers between devices with their start and end apart: 6, of which 3 were waited for; matrix products, arithmetic and copies ran while one was open for 17% of the time, Pallas kernels for 0%

commit v1 on v0

--- a/solution.py
+++ b/solution.py
@@ -93,9 +93,8 @@
     act_sig = jax.nn.sigmoid(shifted)
     swished = (shifted * act_sig * live_rows).astype(jnp.bfloat16)
     dshift = live_rows * dswish * act_sig * (1.0 + shifted * (1.0 - act_sig))
-    sum_gain, sum_bias = lax.psum(
-        (jnp.sum(dshift * normed, axis=0), jnp.sum(dshift, axis=0)), ("dp", "tm")
-    )
+    assign_surface = lambda my_data: lax.psum(lax.psum(my_data, "tm"), "dp")
+    sum_gain, sum_bias = assign_surface((jnp.sum(dshift * normed, axis=0), jnp.sum(dshift, axis=0)))
     dconv = (
         live_rows * bn_gain * inv_std * (dshift - sum_bias / count - normed * sum_gain / count)
     ).astype(jnp.bfloat16)

time: 604 us -> 589 us (0.975)
  blocking collectives: 133 us -> 122 us
    psum x1 -> x2, blocking collectives: 63.8 us -> 52.6 us  [local(): assign_surface = lambda my_data: lax.psum(lax.psum(my_data, 'tm'), 'dp')]
where the time goes in v1:
time: 589 us
  waiting for transfers between devices  281 us (48%)
  blocking collectives  122 us (21%)
  other arithmetic  111 us (19%)
  matrix products  30 us (5%)
  local copies, waits for them, and re-layouts  22.3 us (4%)
  between operations  15.2 us (3%)
  starting transfers between devices  7.12 us (1%)
    unnamed x3, waiting for transfers between devices  223 us
    psum x1, blocking collectives, local(): lax.psum((local_sum, local_sq, local_count), ('dp', 'tm'))  69.6 us
    psum x1, waiting for transfers between devices, local(): lax.psum(taps_kernel(padded, dconv, kernel_taps, frame_rows), ('dp', 'tm'))  54.2 us
    psum x2, blocking collectives, local(): assign_surface = lambda my_data: lax.psum(lax.psum(my_data, 'tm'), 'dp')  52.6 us
    another operation x2, other arithmetic  44.7 us
    reduce_sum x5, other arithmetic, taps_kernel(): jnp.sum(padded_glu[tap_index:tap_index + frame_count].astype(jnp.float32)...  27.5 us
    reduce_sum x1, other arithmetic, local(): local_sum = jnp.sum(conv_out * live_rows, axis=0)  24.4 us
    dot_general x4, matrix products, row_product(): lax.dot_general(left_rows, right_mat, dim_spec, preferred_element_type=jn...  22 us
  transfers between devices with their start and end apart: 6, of which 3 were waited for; matrix products, arithmetic and copies ran while one was open for 17% of the time, Pallas kernels for 0%

profile of v1, /device:TPU:0, one launch (start us, length us, event | category | flops | bytes accessed | tf_op | source)
XLA Modules:
  0.0 588.6 jit_solution(4118596936792861598)
XLA Ops:
  8.0 5.7 fusion.143
  14.6 1.8 copy-done.4
  16.4 1.4 collective-permute-start
  17.8 1.3 collective-permute-start.1
  19.8 3.0 collective-permute-done.1
  22.8 24.4 %multiply_reduce_fusion.2 = (f32[1024]{0:T(1024)S(1)}, f32[1024]{0:T(1024)S(1)}, f32[768,1024]{1,0:T(8,128)}) fusion(f32[768]{0:T(1024)S(1)} %fusion.147, bf16[15,1024]{1,0:T(8,128)(2,1)S(1)} %collective-permute-done.1, bf16[768,1024]{1,0:T(8,128)(2,1)S(1)} %multiply_convert_fusion.4, f32[1024]{0:T(1024)S(1)} %bitcast.146, f32[1024]{0:T(1024)S(1)} %bitcast.148, ...), kind=kLoop, calls=%fused_computation.213 | loop fusion | flops 147060736 | bytes 4918272 | tf_op jit(solution)/shard_map/reduce_sum | solution.py:84
  47.2 69.6 %all-reduce = (f32[1024]{0:T(1024)S(1)}, f32[]{:T(128)}, f32[1024]{0:T(1024)S(1)}) all-reduce(f32[1024]{0:T(1024)S(1)} %get-tuple-element.52, f32[]{:T(128)} %fusion.148, f32[1024]{0:T(1024)S(1)} %get-tuple-element.51), channel_id=1, replica_groups=mesh['dp'=16,'tm'=8] {'dp','tm'}, use_global_device_ids=true, to_apply=%region_5.0 | all-reduce | flops 2049 | bytes 16392 | tf_op jit(solution)/shard_map/psum | solution.py:87
  117.5 6.4 %fusion.151 = (f32[1024]{0:T(1024)S(1)}, f32[1024]{0:T(1024)S(1)}, f32[768,1024]{1,0:T(8,128)}) fusion(f32[1024]{0:T(1024)S(1)} %get-tuple-element.108, f32[768,1024]{1,0:T(8,128)} %get-tuple-element.69, f32[1024]{0:T(1024)S(1)} %get-tuple-element.107, f32[1024]{0:T(1024)S(1)} %copy-done.16, f32[1024]{0:T(1024)S(1)} %copy-done.12, ...), kind=kOutput, calls=%fused_computation.316 | convolution fusion | flops 1623193600 | bytes 9989120 | tf_op jit(solution)/shard_map/dot_general | solution.py:60
  124.0 13.8 %all-reduce.2 = (f32[1024]{0:T(1024)S(1)}, f32[1024]{0:T(1024)S(1)}) all-reduce(f32[1024]{0:T(1024)S(1)} %get-tuple-element.58, f32[1024]{0:T(1024)S(1)} %get-tuple-element.57), channel_id=1, replica_groups=mesh['dp'=16,'tm'=8] {'tm'}, use_global_device_ids=true, to_apply=%region_10.0 | all-reduce | flops 2048 | bytes 16384 | tf_op jit(solution)/shard_map/psum | solution.py:96
  137.8 38.8 %all-reduce.1 = (f32[1024]{0:T(1024)S(1)}, f32[1024]{0:T(1024)S(1)}) all-reduce(f32[1024]{0:T(1024)S(1)} %get-tuple-element.64, f32[1024]{0:T(1024)S(1)} %get-tuple-element.65), channel_id=1, replica_groups=mesh['dp'=16,'tm'=8] {'dp'}, use_global_device_ids=true, to_apply=%region_11.0 | all-reduce | flops 2048 | bytes 16384 | tf_op jit(solution)/shard_map/psum | solution.py:96
  176.6 1.2 broadcast_multiply_fusion.3
  177.8 15.0 %fusion.75 = (f32[1024]{0:T(1024)S(1)}, f32[1024]{0:T(1024)S(1)}, f32[1024]{0:T(1024)S(1)}, f32[1024]{0:T(1024)S(1)}, f32[1024]{0:T(1024)S(1)}, /*index=5*/f32[1024]{0:T(1024)S(1)}, bf16[768,1024]{1,0:T(8,128)(2,1)S(1)}) fusion(bf16[15,1024]{1,0:T(8,128)(2,1)S(1)} %collective-permute-done.1, bf16[768,1024]{1,0:T(8,128)(2,1)} %copy-done.1, ...), kind=kLoop, calls=%fused_computation.196 | loop fusion | flops 36956160 | bytes 9516036 | tf_op jit(solution)/shard_map/reduce_sum | solution.py:50
  192.9 1.3 collective-permute-start.2
  194.2 3.0 collective-permute-start.3
  197.2 2.7 fusion.60
  199.9 3.2 fusion.74
  203.2 2.9 fusion.59
  206.1 3.7 fusion.76
  209.8 4.5 fusion.139
  214.3 2.7 stack.127
  217.0 40.0 %multiply_convert_fusion.1 = (bf16[768,1024]{1,0:T(8,128)(2,1)S(1)}, f32[768,1024]{1,0:T(8,128)S(1)}) fusion(f32[768,2048]{1,0:T(8,128)} %copy-done.4, bf16[768,1024]{1,0:T(8,128)(2,1)} %copy-done.3, bf16[15,1024]{1,0:T(8,128)(2,1)S(1)} %collective-permute-done.3, f32[1024]{0:T(1024)S(1)} %bitcast.147, f32[1024]{0:T(1024)S(1)} %bitcast.149, ...), kind=kLoop, calls=%fused_computation.204 | loop fusion | flops 147849216 | bytes 9628672 | tf_op jit(solution)/shard_map/convert
  257.0 4.7 multiply_convert_fusion
  261.8 3.5 convolution_bitcast_fusion
  265.3 8.0 %pad_maximum_fusion = f32[1024,3072]{0,1:T(8,128)} fusion(f32[1024,1024]{0,1:T(8,128)S(1)} %copy-done.6, f32[1024,2048]{0,1:T(8,128)S(1)} %convolution_bitcast_fusion), kind=kLoop, calls=%fused_computation.32 | loop fusion | flops 3145728 | bytes 25165824 | tf_op jit(solution)/shard_map/concatenate | solution.py:113
  273.3 12.6 %copy.19 = f32[1024,3072]{1,0:T(8,128)} copy(f32[1024,3072]{0,1:T(8,128)} %pad_maximum_fusion) | data formatting | bytes 25165824
  286.5 5.4 fusion.146
  291.9 4.6 fusion.145
  296.5 54.2 %all-reduce.5.cloned.1.call-done = f32[31,1024]{1,0:T(8,128)} async-done(((f32[31,1024]{1,0:T(8,128)}), f32[31,1024]{1,0:T(8,128)}) %all-reduce.5.cloned.1.call-update) | async-done | bytes 126992 | tf_op jit(solution)/shard_map/psum | solution.py:103
  350.7 1.6 broadcast_multiply_fusion.2
  352.3 223.3 %reduce-scatter.4.cloned.1.call-done = f32[8,3072]{1,0:T(8,128)} async-done(((f32[1024,3072]{1,0:T(8,128)}), f32[8,3072]{1,0:T(8,128)}) %reduce-scatter.4.cloned.1.call-update) | async-done | bytes 98320
  578.5 1.1 broadcast_multiply_fusion
  579.6 2.2 copy.17
  (55 shorter events, 6.0 us)
Async XLA Ops:
  7.2 110.4 %copy-start = (bf16[1024,1024]{1,0:T(8,128)(2,1)S(1)}, bf16[1024,1024]{1,0:T(8,128)(2,1)}, u32[]{:S(2)}) copy-start(bf16[1024,1024]{1,0:T(8,128)(2,1)} %param.14) | copy-start | bytes 6291460
  7.2 343.5 %all-reduce.5.cloned.1.call-start = ((), (), s32[]{:S(2)}) async-start(), calls=%async_computation.1 | async-start | bytes 262144 | tf_op jit(solution)/shard_map/psum | solution.py:103
  13.7 2.7 copy-start.4
  13.7 5.4 copy-start.11
  16.4 6.4 %copy-start.1 = (bf16[768,1024]{1,0:T(8,128)(2,1)}, bf16[768,1024]{1,0:T(8,128)(2,1)S(1)}, u32[]{:S(2)}) copy-start(bf16[768,1024]{1,0:T(8,128)(2,1)S(1)} %multiply_convert_fusion.4) | copy-start | bytes 4718596
  16.4 101.2 %copy-start.12 = (f32[1024]{0:T(1024)S(1)}, f32[1024]{0:T(1024)}, u32[]{:S(2)}) copy-start(f32[1024]{0:T(1024)} %param.12) | copy-start | bytes 12292
  16.4 101.2 %copy-start.16 = (f32[1024]{0:T(1024)S(1)}, f32[1024]{0:T(1024)}, u32[]{:S(2)}) copy-start(f32[1024]{0:T(1024)} %param.13) | copy-start | bytes 12292
  16.4 3.5 collective-permute-start
  17.8 5.0 collective-permute-start.1
  177.8 19.4 %copy-start.2 = (bf16[768,1024]{1,0:T(8,128)(2,1)S(1)}, bf16[768,1024]{1,0:T(8,128)(2,1)}, u32[]{:S(2)}) copy-start(bf16[768,1024]{1,0:T(8,128)(2,1)} %copy-done.1) | copy-start | bytes 4718596
  192.9 13.2 %copy-start.3 = (bf16[768,1024]{1,0:T(8,128)(2,1)}, bf16[768,1024]{1,0:T(8,128)(2,1)S(1)}, u32[]{:S(2)}) copy-start(bf16[768,1024]{1,0:T(8,128)(2,1)S(1)} %get-tuple-element.66) | copy-start | bytes 4718596
  192.9 24.1 %collective-permute-start.2 = (bf16[15,1024]{1,0:T(8,128)(2,1)S(1)}, bf16[15,1024]{1,0:T(8,128)(2,1)S(1)}, u32[]{:S(2)}, u32[]{:S(2)}) collective-permute-start(bf16[15,1024]{1,0:T(8,128)(2,1)S(1)} %get-tuple-element.70), channel_id=1, source_target_pairs={{1,0},{2,1},{3,2},{4,3},{5,4},{6,5},{7,6},{9,8},{10,9},{11,10},{12... | collective-permute-start | bytes 92168 | tf_op jit(solution)/shard_map/ppermute | solution.py:18
  194.2 22.8 %collective-permute-start.3 = (bf16[15,1024]{1,0:T(8,128)(2,1)S(1)}, bf16[15,1024]{1,0:T(8,128)(2,1)S(1)}, u32[]{:S(2)}, u32[]{:S(2)}) collective-permute-start(bf16[15,1024]{1,0:T(8,128)(2,1)S(1)} %get-tuple-element.71), channel_id=1, source_target_pairs={{0,1},{1,2},{2,3},{3,4},{4,5},{5,6},{6,7},{8,9},{9,10},{10,11},{11... | collective-permute-start | bytes 92168 | tf_op jit(solution)/shard_map/ppermute | solution.py:16
  203.1 6.6 %copy-start.5 = (f32[768,1024]{1,0:T(8,128)S(1)}, f32[768,1024]{1,0:T(8,128)}, u32[]{:S(2)}) copy-start(f32[768,1024]{1,0:T(8,128)} %get-tuple-element.69) | copy-start | bytes 9437188
  203.1 6.6 %copy-start.14 = (bf16[1,768,1024]{2,1,0:T(8,128)(2,1)S(1)}, bf16[1,768,1024]{2,1,0:T(8,128)(2,1)}, u32[]{:S(2)}) copy-start(bf16[1,768,1024]{2,1,0:T(8,128)(2,1)} %param.15) | copy-start | bytes 4718596
  216.9 358.6 %reduce-scatter.4.cloned.1.call-start = ((), (), s32[]{:S(2)}) async-start(), calls=%async_computation.2 | async-start | bytes 12681216
  257.0 4.7 copy-start.7
  257.0 4.7 copy-start.15
  261.7 3.5 copy-start.9
  261.7 3.5 copy-start.6
  286.5 5.4 copy-start.8
  286.5 5.4 copy-start.10
  286.5 5.4 copy-start.13
Sparse Core Ops, SparseCore 0:
  217.1 133.5 all-reduce.4
  356.4 219.0 reduce-scatter.3
